TPU v7x, 512 devices: a whole 4x8x8 slice. The times are simulated.
512 devices in a mesh: rows: 64 (over x, z, core), cols: 8 (over y).
Axes of the slice: x: 4, y: 8, z: 8, core: 2. Of those that a mesh axis runs over, the one named last changes fastest.
Arguments:
- sample_embeddings: bfloat16 [131072, 256], P(('rows', 'cols')), may hold values from -0.5 to 0.5
- reference_embeddings: bfloat16 [8192, 256], P(('cols', 'rows')), may hold values from -0.5 to 0.5
- sample_mass: float32 [131072], P('rows'), may hold values from 0.05 to 20
- reference_mass: float32 [8192], P('cols'), may hold values from 0.05 to 20
- start_potential: float32 [8192], P('cols'), may hold values from -1.5 to 31.7
- tile_pairs: int32 [64, 8, 2, 48], P('rows', 'cols'), may hold values from 0 to 15, as said below
- tile_counts: int32 [64, 8], P('rows', 'cols'), may hold values from 16 to 48, as said below
Outputs:
- sample_potential: float32 [131072], P('rows')
- reference_potential: float32 [8192], P('cols')
Inputs may be any that keep to these rules, and one draw needn't show every extreme that they name: tile_pairs[a, b, 0, t] is a row tile (below 16) and tile_pairs[a, b, 1, t] a column tile (below 8) of device (a, b); only the first tile_counts[a, b] slots are in use, the rest hold other valid pairs; used pairs of a device are distinct, and every row tile and every column tile of a device appears among its used pairs. `tile_counts`: some device uses all 48 slots in every draw.
All inputs are finite; a program needn't handle non-finite values.
Results may differ from a plain program's by a relative error of at most 0.0003.
Values may be sent and summed in bfloat16 or wider, within the bound.
A program may use at most 64 MiB of HBM per device.

v0:
```python
import jax
import jax.numpy as jnp
from jax import lax
from jax.sharding import PartitionSpec as P

TILE = 128
ITERS = 2


entropy = 0.1
lowest = -1e30
per_block = 4


def onehot_rows(index_list, extent):
    return (index_list[:, None] == jnp.arange(extent, dtype=jnp.int32)[None, :]).astype(jnp.float32)


def select(onehot, lookup_table):
    return jnp.einsum("tn,nk->tk", onehot, lookup_table, precision=lax.Precision.HIGHEST)


def local_pass(
    row_stack, column_stack, row_norms, column_norms, pairs, in_use, potential, along_rows
):
    row_count = row_stack.shape[0]
    column_count = column_stack.shape[0]
    target = row_count if along_rows else column_count

    def advance(block, state):
        peak, total = state
        slots_here = block * per_block + jnp.arange(per_block, dtype=jnp.int32)
        usable = slots_here < in_use
        row_ids = lax.dynamic_slice_in_dim(pairs[0], block * per_block, per_block)
        column_ids = lax.dynamic_slice_in_dim(pairs[1], block * per_block, per_block)
        inner = lax.dot_general(
            row_stack[row_ids],
            column_stack[column_ids],
            (((2,), (2,)), ((0,), (0,))),
            preferred_element_type=jnp.float32,
        )
        row_onehot = onehot_rows(row_ids, row_count)
        column_onehot = onehot_rows(column_ids, column_count)
        costs = (
            select(row_onehot, row_norms)[:, :, None]
            + select(column_onehot, column_norms)[:, None, :]
            - 2.0 * inner
        )
        if along_rows:
            scores = (select(column_onehot, potential)[:, None, :] - costs) / entropy
            tile_peak = jnp.max(scores, axis=2)
            chosen = row_onehot
        else:
            scores = (select(row_onehot, potential)[:, :, None] - costs) / entropy
            tile_peak = jnp.max(scores, axis=1)
            chosen = column_onehot
        tile_peak = jnp.where(usable[:, None], tile_peak, lowest)
        spread_peaks = jnp.where(chosen[:, :, None] > 0.5, tile_peak[:, None, :], lowest)
        new_peak = jnp.maximum(peak, jnp.max(spread_peaks, axis=0))
        slot_peak = select(chosen, new_peak)
        if along_rows:
            exp_sums = jnp.sum(jnp.exp(scores - slot_peak[:, :, None]), axis=2)
        else:
            exp_sums = jnp.sum(jnp.exp(scores - slot_peak[:, None, :]), axis=1)
        exp_sums = jnp.where(usable[:, None], exp_sums, 0.0)
        added = jnp.einsum("tn,tk->nk", chosen, exp_sums, precision=lax.Precision.HIGHEST)
        return (new_peak, total * jnp.exp(peak - new_peak) + added)

    blocks = (in_use + per_block - 1) // per_block
    start_state = (
        jnp.full((target, TILE), lowest, jnp.float32),
        jnp.zeros((target, TILE), jnp.float32),
    )
    return lax.fori_loop(0, blocks, advance, start_state)


def body(
    sample_embeddings,
    reference_embeddings,
    sample_mass,
    reference_mass,
    start_potential,
    tile_pairs,
    tile_counts,
):
    row_block = lax.all_gather(sample_embeddings, "cols", axis=0, tiled=True)
    column_block = lax.all_gather(reference_embeddings, "rows", axis=0, tiled=True)
    width = row_block.shape[1]
    row_count = row_block.shape[0] // TILE
    column_count = column_block.shape[0] // TILE
    row_stack = row_block.reshape(row_count, TILE, width)
    column_stack = column_block.reshape(column_count, TILE, width)
    row_norms = jnp.sum(jnp.square(row_stack.astype(jnp.float32)), axis=2)
    column_norms = jnp.sum(jnp.square(column_stack.astype(jnp.float32)), axis=2)
    pairs = tile_pairs[0, 0]
    in_use = tile_counts[0, 0]
    row_logs = jnp.log(sample_mass).reshape(row_count, TILE)
    column_logs = jnp.log(reference_mass)
    column_potential = start_potential
    row_potential = row_logs
    for iteration in range(ITERS):
        peak, total = local_pass(
            row_stack,
            column_stack,
            row_norms,
            column_norms,
            pairs,
            in_use,
            column_potential.reshape(column_count, TILE),
            True,
        )
        larger = lax.pmax(peak, "cols")
        total = lax.psum(total * jnp.exp(peak - larger), "cols")
        peak = larger
        row_potential = entropy * row_logs - entropy * (peak + jnp.log(total))
        peak, total = local_pass(
            row_stack, column_stack, row_norms, column_norms, pairs, in_use, row_potential, False
        )
        larger = lax.pmax(peak, "rows")
        total = lax.psum(total * jnp.exp(peak - larger), "rows")
        column_potential = (
            entropy * column_logs.reshape(column_count, TILE) - entropy * (larger + jnp.log(total))
        ).reshape(-1)
    return (row_potential.reshape(-1), column_potential)


def solution(mesh):
    placed = (
        P(("rows", "cols"), None),
        P(("cols", "rows"), None),
        P("rows"),
        P("cols"),
        P("cols"),
        P("rows", "cols", None, None),
        P("rows", "cols"),
    )
    return jax.shard_map(
        body, mesh=mesh, in_specs=placed, out_specs=(P("rows"), P("cols")), check_vma=False
    )
```

profile of v0, /device:TPU:1, one launch (start us, length us, event | category | flops | bytes accessed | tf_op | source)
XLA Modules:
  0.0 796.1 jit_solution(10489406709402615568)
XLA Ops:
  7.2 0.7 all-gather.2.cloned.1.call-update
  8.6 57.7 %all_gather.7 = bf16[1024,256]{1,0:T(8,128)(2,1)S(1)} all-gather(bf16[16,256]{1,0:T(8,128)(2,1)} %param.16), channel_id=1, replica_groups=mesh['rows'=64,'cols'=8] {'rows'}, dimensions={0}, use_global_device_ids=true | all-gather | bytes 532480 | tf_op jit(solution)/shard_map/all_gather | solution.py:87
  66.5 1.7 multiply_reduce_fusion
  68.2 39.4 %while.48 = (s32[]{:T(128)}, f32[16,128]{1,0:T(8,128)S(1)}, f32[16,128]{1,0:T(8,128)S(1)}, s32[]{:T(128)}, s32[2,48]{1,0:T(2,128)S(1)}, /*index=5*/s32[]{:T(128)...) while((s32[]{:T(128)}, f32[16,128]{1,0:T(8,128)S(1)}, ...), condition=%wide.region_6.7_spmd, body=%wide.region_2.6_spmd.sunk | while | flops 34496996 | bytes 2241911 | solution.py:74
  70.4 0.7 add_compare_fusion.8
  74.0 0.7 add_compare_fusion.8
  77.6 0.7 add_compare_fusion.8
  81.2 0.7 add_compare_fusion.8
  84.8 0.7 add_compare_fusion.8
  88.3 0.7 add_compare_fusion.8
  91.9 0.7 add_compare_fusion.8
  95.5 0.7 add_compare_fusion.8
  99.1 0.7 add_compare_fusion.8
  107.7 16.0 %pmax.28 = f32[16,128]{1,0:T(8,128)S(1)} all-reduce(f32[16,128]{1,0:T(8,128)S(1)} %get-tuple-element.238), channel_id=1, replica_groups=mesh['rows'=64,'cols'=8] {'cols'}, use_global_device_ids=true, to_apply=%region_7.8 | all-reduce | flops 2048 | bytes 16384 | tf_op jit(solution)/shard_map/pmax | solution.py:112
  123.7 11.0 %psum.28 = f32[16,128]{1,0:T(8,128)S(1)} all-reduce(f32[16,128]{1,0:T(8,128)S(1)} %exponential_multiply_fusion.1), channel_id=1, replica_groups=mesh['rows'=64,'cols'=8] {'cols'}, use_global_device_ids=true, to_apply=%region_8.9 | all-reduce | flops 2048 | bytes 16384 | tf_op jit(solution)/shard_map/psum | solution.py:113
  134.8 39.3 %while.49 = (s32[]{:T(128)}, f32[8,128]{1,0:T(8,128)S(1)}, f32[8,128]{1,0:T(8,128)S(1)}, s32[]{:T(128)}, s32[2,48]{1,0:T(2,128)S(1)}, /*index=5*/s32[]{:T(128)},...) while((s32[]{:T(128)}, f32[8,128]{1,0:T(8,128)S(1)}, ...), condition=%wide.region_13.14_spmd, body=%wide.region_9.13_spmd.sunk | while | flops 34436452 | bytes 2200887 | solution.py:74
  174.1 132.3 %pmax.29 = f32[8,128]{1,0:T(8,128)S(1)} all-reduce(f32[8,128]{1,0:T(8,128)S(1)} %get-tuple-element.240), channel_id=1, replica_groups=mesh['rows'=64,'cols'=8] {'rows'}, use_global_device_ids=true, to_apply=%region_14.15 | all-reduce | flops 1024 | bytes 8192 | tf_op jit(solution)/shard_map/pmax | solution.py:119
  306.3 123.6 %psum.29 = f32[8,128]{1,0:T(8,128)S(1)} all-reduce(f32[8,128]{1,0:T(8,128)S(1)} %exponential_multiply_fusion.3), channel_id=1, replica_groups=mesh['rows'=64,'cols'=8] {'rows'}, use_global_device_ids=true, to_apply=%region_15.16 | all-reduce | flops 1024 | bytes 8192 | tf_op jit(solution)/shard_map/psum | solution.py:120
  430.0 39.4 %while.50 = (s32[]{:T(128)}, f32[16,128]{1,0:T(8,128)S(1)}, f32[16,128]{1,0:T(8,128)S(1)}, s32[]{:T(128)}, s32[2,48]{1,0:T(2,128)S(1)}, /*index=5*/s32[]{:T(128)...) while((s32[]{:T(128)}, f32[16,128]{1,0:T(8,128)S(1)}, ...), condition=%wide.region_20.21_spmd, body=%wide.region_16.20_spmd.sunk | while | flops 34496996 | bytes 2241911 | solution.py:74
  469.4 15.0 %pmax.30 = f32[16,128]{1,0:T(8,128)S(1)} all-reduce(f32[16,128]{1,0:T(8,128)S(1)} %get-tuple-element.242), channel_id=1, replica_groups=mesh['rows'=64,'cols'=8] {'cols'}, use_global_device_ids=true, to_apply=%region_21.22 | all-reduce | flops 2048 | bytes 16384 | tf_op jit(solution)/shard_map/pmax | solution.py:112
  484.4 13.6 %psum.30 = f32[16,128]{1,0:T(8,128)S(1)} all-reduce(f32[16,128]{1,0:T(8,128)S(1)} %exponential_multiply_fusion), channel_id=1, replica_groups=mesh['rows'=64,'cols'=8] {'cols'}, use_global_device_ids=true, to_apply=%region_22.23 | all-reduce | flops 2048 | bytes 16384 | tf_op jit(solution)/shard_map/psum | solution.py:113
  498.0 39.3 %while.51 = (s32[]{:T(128)}, f32[8,128]{1,0:T(8,128)S(1)}, f32[8,128]{1,0:T(8,128)S(1)}, s32[]{:T(128)}, s32[2,48]{1,0:T(2,128)S(1)}, /*index=5*/s32[]{:T(128)},...) while((s32[]{:T(128)}, f32[8,128]{1,0:T(8,128)S(1)}, ...), condition=%wide.region_27.28_spmd, body=%wide.region_23.27_spmd.sunk | while | flops 34436452 | bytes 2200887 | solution.py:74
  537.3 127.8 %pmax.31 = f32[8,128]{1,0:T(8,128)S(1)} all-reduce(f32[8,128]{1,0:T(8,128)S(1)} %get-tuple-element.244), channel_id=1, replica_groups=mesh['rows'=64,'cols'=8] {'rows'}, use_global_device_ids=true, to_apply=%region_28.29 | all-reduce | flops 1024 | bytes 8192 | tf_op jit(solution)/shard_map/pmax | solution.py:119
  665.1 123.6 %psum.31 = f32[8,128]{1,0:T(8,128)S(1)} all-reduce(f32[8,128]{1,0:T(8,128)S(1)} %exponential_multiply_fusion.2), channel_id=1, replica_groups=mesh['rows'=64,'cols'=8] {'rows'}, use_global_device_ids=true, to_apply=%region_29.30 | all-reduce | flops 1024 | bytes 8192 | tf_op jit(solution)/shard_map/psum | solution.py:120
  (902 shorter events, 149.6 us)
Async XLA Ops:
  7.2 59.3 %all-gather.2.cloned.1.call-start = ((), (), s32[]{:S(2)}) async-start(), calls=%async_computation | async-start | bytes 1179648 | tf_op jit(solution)/shard_map/all_gather | solution.py:86
  8.6 59.6 %copy-start.1 = (s32[1,1,2,48]{3,2,1,0:T(2,128)S(1)}, s32[1,1,2,48]{3,2,1,0:T(2,128)}, u32[]{:S(2)}) copy-start(s32[1,1,2,48]{3,2,1,0:T(2,128)} %param.20) | copy-start | bytes 1156
  8.6 59.6 %copy-start.5 = (f32[1024]{0:T(1024)S(1)}, f32[1024]{0:T(1024)}, u32[]{:S(2)}) copy-start(f32[1024]{0:T(1024)} %param.19) | copy-start | bytes 12292
  66.5 1.7 copy-start
  68.2 66.5 %copy-start.2 = (f32[2048]{0:T(1024)S(1)}, f32[2048]{0:T(1024)}, u32[]{:S(2)}) copy-start(f32[2048]{0:T(1024)} %param.17) | copy-start | bytes 24580
  134.7 295.2 %copy-start.3 = (f32[1024]{0:T(1024)S(1)}, f32[1024]{0:T(1024)}, u32[]{:S(2)}) copy-start(f32[1024]{0:T(1024)} %param.18) | copy-start | bytes 12292
  537.3 252.0 %copy-start.4 = (f32[16,128]{1,0:T(8,128)}, f32[16,128]{1,0:T(8,128)S(1)}, u32[]{:S(2)}) copy-start(f32[16,128]{1,0:T(8,128)S(1)} %get-tuple-element.898) | copy-start | bytes 24580
Sparse Core Ops, SparseCore 0:
  10.1 42.1 all-gather.1
where the time goes:
time: 805 us; the launch traced here: 796 us
  blocking collectives  620 us (77%)
  matrix products  55.1 us (7%)
  local copies, waits for them, and re-layouts  53.8 us (7%)
  other arithmetic  48.2 us (6%)
  between operations  14.9 us (2%)
    pmax x2, blocking collectives, body(): larger = lax.pmax(peak, 'rows')  260 us
    psum x2, blocking collectives, body(): total = lax.psum(total * jnp.exp(peak - larger), 'rows')  247 us
    all_gather x1, blocking collectives, body(): lax.all_gather(reference_embeddings, 'rows', axis=0, tiled=True)  57.7 us
    dot_general x176, matrix products, select(): jnp.einsum('tn,nk->tk', onehot, lookup_table, precision=lax.Precision.HIG...  32.8 us
    pmax x2, blocking collectives, body(): larger = lax.pmax(peak, 'cols')  31 us
    lt x44, other arithmetic, advance(): usable = slots_here < in_use  28.7 us
    gather x44, local copies, waits for them, and re-layouts, advance(): row_stack[row_ids]  25 us
    gather x44, local copies, waits for them, and re-layouts, advance(): column_stack[column_ids]  24.8 us
  transfers between devices with their start and end apart: 1, of which 0 were waited for; matrix products, arithmetic and copies ran while one was open for 0% of the time, Pallas kernels for 0%

commit v1 on v0

v1 whole, which is shorter than its diff:
```python
import math

import jax
import jax.numpy as jnp
from jax import lax
from jax.experimental import pallas as pl
from jax.experimental.pallas import tpu as pltpu
from jax.sharding import PartitionSpec as P

TILE = 128
ITERS = 2
WIDTH = 256
ROW_TILES = 16
COLUMN_TILES = 8
SLOTS = 48
PIECES = 4
FAR_FIRST = (4, 3, 5, 2, 6, 1, 7)

SCALE = math.log2(math.e) / 0.1
LOWEST = -1e30
MESH = pl.DeviceIdType.MESH


def remote(source, target, send_sem, recv_sem, device):
    return pltpu.make_async_remote_copy(
        src_ref=source,
        dst_ref=target,
        send_sem=send_sem,
        recv_sem=recv_sem,
        device_id=device,
        device_id_type=MESH,
    )


def tile_norms(load_tile, count):
    padded = max(count, 16)
    ones = jnp.ones((padded, WIDTH), jnp.bfloat16)
    place = lax.broadcasted_iota(jnp.int32, (padded, TILE), 0)

    def one(tile, found):
        values = load_tile(tile).astype(jnp.float32)
        squares = values * values
        high = squares.astype(jnp.bfloat16)
        low = (squares - high.astype(jnp.float32)).astype(jnp.bfloat16)
        sums = dot_rows(ones, high) + dot_rows(ones, low)
        return jnp.where(place == tile, sums, found)

    found = lax.fori_loop(0, count, one, jnp.zeros((padded, TILE), jnp.float32))
    return found[:count]


def dot_rows(left, right):
    return lax.dot_general(
        left, right, (((1,), (1,)), ((), ())), preferred_element_type=jnp.float32
    )


def spread(values, spread_ref):
    turned = values.T
    for tile in range(values.shape[0]):
        spread_ref[tile] = jnp.broadcast_to(turned[:, tile : tile + 1], (TILE, TILE))


def log_sum(parts):
    peak = jnp.max(parts, axis=0)
    return peak + jnp.log2(jnp.sum(jnp.exp2(parts - peak[None]), axis=0))


def kernel(
    samples,
    references,
    sample_mass,
    reference_mass,
    start,
    pairs,
    counts,
    sample_out,
    reference_out,
    row_buf,
    column_buf,
    column_major,
    row_major,
    column_spread,
    row_spread,
    slot_peak,
    slot_total,
    row_bias,
    column_bias,
    y_buf,
    x_buf,
    z_buf,
    own_sem,
    ring_send,
    ring_recv,
    gather_send,
    gather_recv,
    y_send,
    y_recv,
    x_send,
    x_recv,
    z_send,
    z_recv,
):
    row = lax.axis_index("rows")
    y = lax.axis_index("cols")
    x = lax.div(row, 16)
    z = lax.rem(lax.div(row, 2), 8)
    core = lax.rem(row, 2)
    corner = x * 2 + core

    def at(px, pz, pcore):
        return ((px * 8 + pz) * 2 + pcore, y)

    def y_peer(step):
        return (row, lax.rem(y + step, 8))

    def z_peer(step):
        return at(x, lax.rem(z + step, 8), core)

    def corner_peer(step):
        other = lax.rem(corner + step, 8)
        return at(lax.div(other, 2), z, lax.rem(other, 2))

    barrier = pltpu.get_barrier_semaphore()
    for step in FAR_FIRST:
        for peer in (y_peer(step), z_peer(step), corner_peer(step)):
            pl.semaphore_signal(barrier, inc=1, device_id=peer, device_id_type=MESH)

    def block_of(px, pz, pcore):
        return column_buf.at[px * 2 + lax.div(pz, 4), lax.rem(pz, 4), pcore]

    own_copies = [
        pltpu.make_async_copy(
            samples.at[pl.ds(64 * piece, 64)],
            row_buf.at[2 * y + piece // 2, piece % 2],
            own_sem.at[piece],
        )
        for piece in range(PIECES)
    ]
    own_copies.append(
        pltpu.make_async_copy(references, block_of(x, z, core), own_sem.at[PIECES])
    )
    for copy in own_copies:
        copy.start()

    in_use = counts[0, 0]
    row_place = lax.broadcasted_iota(jnp.int32, (ROW_TILES, TILE), 0)
    column_place = lax.broadcasted_iota(jnp.int32, (COLUMN_TILES, TILE), 0)

    def mark(slot, carry):
        spare = jnp.where(slot < in_use, 0.0, LOWEST).astype(jnp.float32)
        row_bias[slot] = jnp.where(row_place == pairs[0, 0, 0, slot], spare, LOWEST)
        column_bias[slot] = jnp.where(column_place == pairs[0, 0, 1, slot], spare, LOWEST)
        return carry

    lax.fori_loop(0, SLOTS, mark, 0)

    pl.semaphore_wait(barrier, 21)

    z_copies = []
    for step in FAR_FIRST:
        copy = remote(
            references,
            block_of(x, z, core),
            gather_send.at[step],
            gather_recv.at[step],
            z_peer(step),
        )
        copy.start()
        z_copies.append(copy)

    ring = {}

    def ring_start(hop, piece):
        for side in (0, 1):
            if hop == 4 and (piece < 2) != (side == 0):
                continue
            back = hop - 1
            block = lax.rem(y + (8 - back if side == 0 else back), 8)
            landing = row_buf.at[2 * block + piece // 2, piece % 2]
            source = samples.at[pl.ds(64 * piece, 64)] if hop == 1 else landing
            copy = remote(
                source,
                landing,
                ring_send.at[side, hop - 1, piece],
                ring_recv.at[side, hop - 1, piece],
                y_peer(1 if side == 0 else 7),
            )
            copy.start()
            ring[side, hop, piece] = copy

    def ring_wait(hop, piece):
        for side in (0, 1):
            if (side, hop, piece) in ring:
                ring[side, hop, piece].wait_recv()

    for piece in range(PIECES):
        ring_start(1, piece)
    for piece in range(PIECES):
        ring_wait(1, piece)
        ring_start(2, piece)

    for copy in own_copies:
        copy.wait()
    for copy in z_copies:
        copy.wait_recv()
    x_copies = []
    for step in (2, 1, 3):
        mine = column_buf.at[pl.ds(2 * x, 2), :, core]
        copy = remote(
            mine,
            mine,
            gather_send.at[7 + step],
            gather_recv.at[7 + step],
            at(lax.rem(x + step, 4), z, core),
        )
        copy.start()
        x_copies.append(copy)

    for piece in range(PIECES):
        ring_wait(2, piece)
        ring_start(3, piece)
    for piece in range(PIECES):
        ring_wait(3, piece)
        ring_start(4, piece)

    for copy in x_copies:
        copy.wait_recv()
    mine = column_buf.at[:, :, core]
    core_copy = remote(
        mine, mine, gather_send.at[11], gather_recv.at[11], at(x, z, 1 - core)
    )
    core_copy.start()
    core_copy.wait_recv()

    def row_tile(tile):
        return row_buf[tile].reshape(TILE, WIDTH)

    def column_tile(tile):
        return column_buf[tile].reshape(TILE, WIDTH)

    column_norms = tile_norms(column_tile, COLUMN_TILES)
    spread(SCALE * (start[...] - column_norms), column_spread)

    for piece in range(PIECES):
        ring_wait(4, piece)

    def multiply(slot, carry):
        row_values = row_tile(pairs[0, 0, 0, slot])
        column_values = column_tile(pairs[0, 0, 1, slot])
        column_major[slot] = (2.0 * SCALE) * dot_rows(column_values, row_values)
        row_major[slot] = (2.0 * SCALE) * dot_rows(row_values, column_values)
        return carry

    lax.fori_loop(0, SLOTS, multiply, 0, unroll=2)

    def local_pass(products, spread_ref, axis, bias):
        def one(slot, carry):
            scores = products[slot] + spread_ref[pairs[0, 0, axis, slot]]
            peak = jnp.max(scores, axis=0, keepdims=True)
            slot_peak[pl.ds(slot, 1), :] = peak
            slot_total[pl.ds(slot, 1), :] = jnp.sum(
                jnp.exp2(scores - peak), axis=0, keepdims=True
            )
            return carry

        lax.fori_loop(0, SLOTS, one, 0, unroll=4)
        slot_peak[...] = slot_peak[...] + jnp.log2(slot_total[...])

        shape = bias.shape[1:]

        def highest(slot, peak):
            return jnp.maximum(peak, slot_peak[pl.ds(slot, 1), :] + bias[slot])

        peak = lax.fori_loop(
            0, SLOTS, highest, jnp.full(shape, LOWEST, jnp.float32), unroll=8
        )

        def collect(slot, total):
            return total + jnp.exp2(slot_peak[pl.ds(slot, 1), :] + bias[slot] - peak)

        total = lax.fori_loop(
            0, SLOTS, collect, jnp.zeros(shape, jnp.float32), unroll=8
        )
        return peak + jnp.log2(total)

    def exchange(value, buf, iteration, place, peer, send_sem, recv_sem):
        buf[iteration, place] = value
        copies = []
        for step in FAR_FIRST:
            mine = buf.at[iteration, place]
            copy = remote(
                mine,
                mine,
                send_sem.at[iteration, step],
                recv_sem.at[iteration, step],
                peer(step),
            )
            copy.start()
            copies.append(copy)
        return copies

    def finish(copies, buf, iteration):
        for copy in copies:
            copy.wait()
        return log_sum(buf[iteration])

    sample_logs = jnp.log2(sample_mass[...])
    reference_logs = jnp.log2(reference_mass[...])
    for iteration in range(ITERS):
        value = local_pass(column_major, column_spread, 1, row_bias)
        copies = exchange(value, y_buf, iteration, y, y_peer, y_send, y_recv)
        if iteration == 0:
            row_norms = tile_norms(row_tile, ROW_TILES)
        row_level = sample_logs - finish(copies, y_buf, iteration)
        spread(row_level, row_spread)
        if iteration == ITERS - 1:
            sample_out[...] = row_level * (1.0 / SCALE) + row_norms
        value = local_pass(row_major, row_spread, 0, column_bias)
        copies = exchange(value, x_buf, iteration, corner, corner_peer, x_send, x_recv)
        value = finish(copies, x_buf, iteration)
        copies = exchange(value, z_buf, iteration, z, z_peer, z_send, z_recv)
        column_level = reference_logs - finish(copies, z_buf, iteration)
        if iteration < ITERS - 1:
            spread(column_level, column_spread)
        else:
            reference_out[...] = column_level * (1.0 / SCALE) + column_norms

    for copy in ring.values():
        copy.wait_send()
    for copy in z_copies + x_copies + [core_copy]:
        copy.wait_send()


def body(
    sample_embeddings,
    reference_embeddings,
    sample_mass,
    reference_mass,
    start_potential,
    tile_pairs,
    tile_counts,
):
    vmem = pl.BlockSpec(memory_space=pltpu.VMEM)
    smem = pl.BlockSpec(memory_space=pltpu.SMEM)
    anywhere = pl.BlockSpec(memory_space=pl.ANY)
    dma = pltpu.SemaphoreType.DMA
    sample_out, reference_out = pl.pallas_call(
        kernel,
        out_shape=(
            jax.ShapeDtypeStruct((ROW_TILES, TILE), jnp.float32),
            jax.ShapeDtypeStruct((COLUMN_TILES, TILE), jnp.float32),
        ),
        in_specs=[anywhere, anywhere, vmem, vmem, vmem, smem, smem],
        out_specs=(vmem, vmem),
        scratch_shapes=[
            pltpu.VMEM((ROW_TILES, 2, 64, WIDTH), jnp.bfloat16),
            pltpu.VMEM((COLUMN_TILES, 4, 2, 16, WIDTH), jnp.bfloat16),
            pltpu.VMEM((SLOTS, TILE, TILE), jnp.float32),
            pltpu.VMEM((SLOTS, TILE, TILE), jnp.float32),
            pltpu.VMEM((COLUMN_TILES, TILE, TILE), jnp.float32),
            pltpu.VMEM((ROW_TILES, TILE, TILE), jnp.float32),
            pltpu.VMEM((SLOTS, TILE), jnp.float32),
            pltpu.VMEM((SLOTS, TILE), jnp.float32),
            pltpu.VMEM((SLOTS, ROW_TILES, TILE), jnp.float32),
            pltpu.VMEM((SLOTS, COLUMN_TILES, TILE), jnp.float32),
            pltpu.VMEM((ITERS, 8, ROW_TILES, TILE), jnp.float32),
            pltpu.VMEM((ITERS, 8, COLUMN_TILES, TILE), jnp.float32),
            pltpu.VMEM((ITERS, 8, COLUMN_TILES, TILE), jnp.float32),
            dma((PIECES + 1,)),
            dma((2, 4, PIECES)),
            dma((2, 4, PIECES)),
            dma((12,)),
            dma((12,)),
            dma((ITERS, 8)),
            dma((ITERS, 8)),
            dma((ITERS, 8)),
            dma((ITERS, 8)),
            dma((ITERS, 8)),
            dma((ITERS, 8)),
        ],
        compiler_params=pltpu.CompilerParams(collective_id=0, has_side_effects=True),
    )(
        sample_embeddings,
        reference_embeddings,
        sample_mass.reshape(ROW_TILES, TILE),
        reference_mass.reshape(COLUMN_TILES, TILE),
        start_potential.reshape(COLUMN_TILES, TILE),
        tile_pairs,
        tile_counts,
    )
    return (sample_out.reshape(-1), reference_out.reshape(-1))


def solution(mesh):
    placed = (
        P(("rows", "cols"), None),
        P(("cols", "rows"), None),
        P("rows"),
        P("cols"),
        P("cols"),
        P("rows", "cols", None, None),
        P("rows", "cols"),
    )
    return jax.shard_map(
        body, mesh=mesh, in_specs=placed, out_specs=(P("rows"), P("cols")), check_vma=False
    )
```

time: 805 us -> 73.6 us (0.09); the launches traced: 796 us -> 73.3 us
  blocking collectives: 620 us -> 0 us
  Pallas kernels: 0 us -> 70.2 us
  matrix products: 55.1 us -> 0 us
  local copies, waits for them, and re-layouts: 53.8 us -> 1.89 us
  other arithmetic: 48.2 us -> 0 us
  between operations: 14.9 us -> 1.3 us
    pmax x4 -> x0, blocking collectives: 291 us -> none  [the longest x2 260 us: body(): larger = lax.pmax(peak, 'rows')]
    psum x4 -> x0, blocking collectives: 272 us -> none  [the longest x2 247 us: body(): total = lax.psum(total * jnp.exp(peak - larger), 'rows')]
    pallas_call x0 -> x1, Pallas kernels: none -> 70.2 us  [body(): pl.pallas_call(kernel, out_shape=(jax.ShapeDtypeStruct((ROW_TILES, TILE),...]
    all_gather x1 -> x0, blocking collectives: 57.7 us -> none  [body(): lax.all_gather(reference_embeddings, 'rows', axis=0, tiled=True)]
    dot_general x264 -> x0, matrix products: 55.1 us -> none  [the longest x176 32.8 us: select(): jnp.einsum('tn,nk->tk', onehot, lookup_table, precision=lax.Precision.HIG...]
    gather x88 -> x0, local copies, waits for them, and re-layouts: 49.8 us -> none  [the longest x44 25 us: advance(): row_stack[row_ids]]
    lt x44 -> x0, other arithmetic: 28.7 us -> none  [advance(): usable = slots_here < in_use]
  transfers between devices with their start and end apart: 1 -> 0, of which waited for: 0 -> 0; matrix products, arithmetic and copies ran while one was open for 0% -> 0% of each run, Pallas kernels for 0% -> 0%
where the time goes in v1:
time: 73.6 us; the launch traced here: 73.3 us
  Pallas kernels  70.2 us (95%)
  local copies, waits for them, and re-layouts  1.89 us (3%)
  between operations  1.3 us (2%)
    pallas_call x1, Pallas kernels, body(): pl.pallas_call(kernel, out_shape=(jax.ShapeDtypeStruct((ROW_TILES, TILE),...  70.2 us
    unnamed x4, local copies, waits for them, and re-layouts  1.89 us

profile of v1, /device:TPU:1, one launch (start us, length us, event | category | flops | bytes accessed | tf_op | source)
XLA Modules:
  0.0 73.3 jit_solution(17596538545534874589)
XLA Ops:
  1.3 70.2 %shard_map.86 = (f32[16,128]{1,0:T(8,128)}, f32[8,128]{1,0:T(8,128)}) custom-call(bf16[256,256]{1,0:T(8,128)(2,1)} %samples.1, bf16[16,256]{1,0:T(8,128)(2,1)} %references.1, f32[16,128]{1,0:T(8,128)} %bitcast.5, f32[8,128]{1,0:T(8,128)} %bitcast.7, f32[8,128]{1,0:T(8,128)} %bitcast.8, s32[1,1,2,48]{3,2,1,0:T(2,128)} %pairs.1, s32[1,1]{1,0:T(1,128)S(6)} %copy.11.counts), custom_call_target="tpu_custom_call" | custom-call | tf_op jit(solution)/shard_map/pallas_call | solution.py:348
  71.4 0.0 copy-start
  71.4 1.3 %copy.12 = f32[2048]{0:T(1024)} copy(f32[2048]{0:T(1024)} %bitcast.6) | data formatting | bytes 16384
  72.7 0.0 copy-done
  72.7 0.6 copy.13
Async XLA Ops:
  71.4 1.3 %copy-start = (f32[8,128]{1,0:T(8,128)S(1)}, f32[8,128]{1,0:T(8,128)}, u32[]{:S(2)}) copy-start(f32[8,128]{1,0:T(8,128)} %get-tuple-element.5) | copy-start | bytes 12292

commit v2 on v1

--- a/solution.py
+++ b/solution.py
@@ -157,81 +157,74 @@
 
     pl.semaphore_wait(barrier, 21)
 
-    z_copies = []
-    for step in FAR_FIRST:
-        copy = remote(
-            references,
-            block_of(x, z, core),
-            gather_send.at[step],
-            gather_recv.at[step],
-            z_peer(step),
-        )
+    def gather(source, target, index, device):
+        copy = remote(source, target, gather_send.at[*index], gather_recv.at[*index], device)
         copy.start()
-        z_copies.append(copy)
+        return copy
+
+    z_copies = {
+        step: gather(references, block_of(x, z, core), (0, step), z_peer(step))
+        for step in (1, 7, 2, 6, 3, 5, 4)
+    }
+    x_copies = {}
+
+    def forward(step):
+        origin = lax.rem(z + (8 - step), 8)
+        landing = block_of(x, origin, core)
+        for x_step in (2, 1, 3):
+            x_copies[x_step, step] = gather(
+                references if step == 0 else landing,
+                landing,
+                (x_step, step),
+                at(lax.rem(x + x_step, 4), z, core),
+            )
 
     ring = {}
 
-    def ring_start(hop, piece):
+    def ring_start(hop, turn):
         for side in (0, 1):
-            if hop == 4 and (piece < 2) != (side == 0):
-                continue
             back = hop - 1
+            piece = turn if side == 0 else PIECES - 1 - turn
             block = lax.rem(y + (8 - back if side == 0 else back), 8)
             landing = row_buf.at[2 * block + piece // 2, piece % 2]
             source = samples.at[pl.ds(64 * piece, 64)] if hop == 1 else landing
             copy = remote(
                 source,
                 landing,
-                ring_send.at[side, hop - 1, piece],
-                ring_recv.at[side, hop - 1, piece],
+                ring_send.at[side, back, turn],
+                ring_recv.at[side, back, turn],
                 y_peer(1 if side == 0 else 7),
             )
             copy.start()
-            ring[side, hop, piece] = copy
-
-    def ring_wait(hop, piece):
+            ring[side, hop, turn] = copy
+
+    def ring_wait(hop, turn):
         for side in (0, 1):
-            if (side, hop, piece) in ring:
-                ring[side, hop, piece].wait_recv()
-
-    for piece in range(PIECES):
-        ring_start(1, piece)
-    for piece in range(PIECES):
-        ring_wait(1, piece)
-        ring_start(2, piece)
-
+            ring[side, hop, turn].wait_recv()
+
+    def ring_turn(hop, turn):
+        ring_wait(hop, turn)
+        if hop < 3 or (hop == 3 and turn < PIECES // 2):
+            ring_start(hop + 1, turn)
+
+    for turn in range(PIECES):
+        ring_start(1, turn)
+    forward(0)
+
+    for turn, steps in enumerate(((1, 7), (2, 6), (3, 5), (4,))):
+        for step in steps:
+            z_copies[step].wait_recv()
+            forward(step)
+        ring_turn(1, turn)
     for copy in own_copies:
         copy.wait()
-    for copy in z_copies:
-        copy.wait_recv()
-    x_copies = []
-    for step in (2, 1, 3):
-        mine = column_buf.at[pl.ds(2 * x, 2), :, core]
-        copy = remote(
-            mine,
-            mine,
-            gather_send.at[7 + step],
-            gather_recv.at[7 + step],
-            at(lax.rem(x + step, 4), z, core),
-        )
-        copy.start()
-        x_copies.append(copy)
-
-    for piece in range(PIECES):
-        ring_wait(2, piece)
-        ring_start(3, piece)
-    for piece in range(PIECES):
-        ring_wait(3, piece)
-        ring_start(4, piece)
-
-    for copy in x_copies:
-        copy.wait_recv()
-    mine = column_buf.at[:, :, core]
-    core_copy = remote(
-        mine, mine, gather_send.at[11], gather_recv.at[11], at(x, z, 1 - core)
-    )
-    core_copy.start()
-    core_copy.wait_recv()
+
+    core_copies = []
+
+    def swap(step):
+        group = lax.rem(x + (4 - step), 4)
+        mine = column_buf.at[pl.ds(2 * group, 2), :, core]
+        core_copies.append(gather(mine, mine, (4, step), at(x, z, 1 - core)))
 
     def row_tile(tile):
         return row_buf[tile].reshape(TILE, WIDTH)
@@ -239,24 +232,57 @@
     def column_tile(tile):
         return column_buf[tile].reshape(TILE, WIDTH)
 
+    def multiply(steps, groups):
+        for step in steps:
+            first = 2 * lax.rem(y + step, 8)
+            row_values = row_buf[pl.ds(first, 2)].reshape(2 * TILE, WIDTH)
+            for group in groups:
+                pair = lax.rem(x + (4 - group), 4)
+                column_values = column_buf[pl.ds(2 * pair, 2)].reshape(2 * TILE, WIDTH)
+                by_column = (2.0 * SCALE) * dot_rows(column_values, row_values)
+                by_row = (2.0 * SCALE) * dot_rows(row_values, column_values)
+                for i in (0, 1):
+                    for j in (0, 1):
+                        rows = slice(i * TILE, (i + 1) * TILE)
+                        columns = slice(j * TILE, (j + 1) * TILE)
+                        place = (first + i) * COLUMN_TILES + 2 * pair + j
+                        column_major[place] = by_column[columns, rows]
+                        row_major[place] = by_row[rows, columns]
+
+    swap(0)
+    ring_turn(2, 0)
+    core_copies[0].wait_recv()
+    multiply((0, 1, 7), (0,))
+    for turn, x_step in enumerate((1, 3, 2)):
+        for step in range(8):
+            x_copies[x_step, step].wait_recv()
+        swap(x_step)
+        ring_turn(2, turn + 1)
+    multiply((2, 6), (0,))
+    core_copies[1].wait_recv()
+    multiply((0, 1, 7), (1,))
+    ring_turn(3, 0)
+    core_copies[2].wait_recv()
+    multiply((0, 1, 7), (3,))
+    ring_turn(3, 1)
+    core_copies[3].wait_recv()
+    multiply((0, 1, 7), (2,))
     column_norms = tile_norms(column_tile, COLUMN_TILES)
     spread(SCALE * (start[...] - column_norms), column_spread)
-
-    for piece in range(PIECES):
-        ring_wait(4, piece)
-
-    def multiply(slot, carry):
-        row_values = row_tile(pairs[0, 0, 0, slot])
-        column_values = column_tile(pairs[0, 0, 1, slot])
-        column_major[slot] = (2.0 * SCALE) * dot_rows(column_values, row_values)
-        row_major[slot] = (2.0 * SCALE) * dot_rows(row_values, column_values)
-        return carry
-
-    lax.fori_loop(0, SLOTS, multiply, 0, unroll=2)
+    ring_turn(3, 2)
+    multiply((2, 6), (1, 2, 3))
+    ring_turn(3, 3)
+    multiply((3, 5), (0, 1, 2, 3))
+    ring_wait(4, 0)
+    ring_wait(4, 1)
+    multiply((4,), (0, 1, 2, 3))
 
     def local_pass(products, spread_ref, axis, bias):
         def one(slot, carry):
-            scores = products[slot] + spread_ref[pairs[0, 0, axis, slot]]
+            row_id = pairs[0, 0, 0, slot]
+            column_id = pairs[0, 0, 1, slot]
+            place = row_id * COLUMN_TILES + column_id
+            scores = products[place] + spread_ref[column_id if axis else row_id]
             peak = jnp.max(scores, axis=0, keepdims=True)
             slot_peak[pl.ds(slot, 1), :] = peak
             slot_total[pl.ds(slot, 1), :] = jnp.sum(
@@ -328,7 +354,7 @@
 
     for copy in ring.values():
         copy.wait_send()
-    for copy in z_copies + x_copies + [core_copy]:
+    for copy in [*z_copies.values(), *x_copies.values(), *core_copies]:
         copy.wait_send()
 
 
@@ -356,8 +382,8 @@
         scratch_shapes=[
             pltpu.VMEM((ROW_TILES, 2, 64, WIDTH), jnp.bfloat16),
             pltpu.VMEM((COLUMN_TILES, 4, 2, 16, WIDTH), jnp.bfloat16),
-            pltpu.VMEM((SLOTS, TILE, TILE), jnp.float32),
-            pltpu.VMEM((SLOTS, TILE, TILE), jnp.float32),
+            pltpu.VMEM((ROW_TILES * COLUMN_TILES, TILE, TILE), jnp.float32),
+            pltpu.VMEM((ROW_TILES * COLUMN_TILES, TILE, TILE), jnp.float32),
             pltpu.VMEM((COLUMN_TILES, TILE, TILE), jnp.float32),
             pltpu.VMEM((ROW_TILES, TILE, TILE), jnp.float32),
             pltpu.VMEM((SLOTS, TILE), jnp.float32),
@@ -370,8 +396,8 @@
             dma((PIECES + 1,)),
             dma((2, 4, PIECES)),
             dma((2, 4, PIECES)),
-            dma((12,)),
-            dma((12,)),
+            dma((5, 8)),
+            dma((5, 8)),
             dma((ITERS, 8)),
             dma((ITERS, 8)),
             dma((ITERS, 8)),

time: 73.6 us -> 69 us (0.938)
  Pallas kernels: 70.2 us -> 65.6 us
    pallas_call x1, Pallas kernels: 70.2 us -> 65.6 us  [body(): pl.pallas_call(kernel, out_shape=(jax.ShapeDtypeStruct((ROW_TILES, TILE),...]
where the time goes in v2:
time: 69 us; the launch traced here: 68.8 us
  Pallas kernels  65.6 us (95%)
  local copies, waits for them, and re-layouts  1.89 us (3%)
  between operations  1.3 us (2%)
    pallas_call x1, Pallas kernels, body(): pl.pallas_call(kernel, out_shape=(jax.ShapeDtypeStruct((ROW_TILES, TILE),...  65.6 us
    unnamed x4, local copies, waits for them, and re-layouts  1.89 us

profile of v2, /device:TPU:1, one launch (start us, length us, event | category | flops | bytes accessed | tf_op | source)
XLA Modules:
  0.0 68.8 jit_solution(6997566796657850696)
XLA Ops:
  1.3 65.6 %shard_map.86 = (f32[16,128]{1,0:T(8,128)}, f32[8,128]{1,0:T(8,128)}) custom-call(bf16[256,256]{1,0:T(8,128)(2,1)} %samples.1, bf16[16,256]{1,0:T(8,128)(2,1)} %references.1, f32[16,128]{1,0:T(8,128)} %bitcast.5, f32[8,128]{1,0:T(8,128)} %bitcast.7, f32[8,128]{1,0:T(8,128)} %bitcast.8, s32[1,1,2,48]{3,2,1,0:T(2,128)} %pairs.1, s32[1,1]{1,0:T(1,128)S(6)} %copy.11.counts), custom_call_target="tpu_custom_call" | custom-call | tf_op jit(solution)/shard_map/pallas_call | solution.py:374
  66.9 0.0 copy-start
  66.9 1.3 %copy.12 = f32[2048]{0:T(1024)} copy(f32[2048]{0:T(1024)} %bitcast.6) | data formatting | bytes 16384
  68.2 0.0 copy-done
  68.2 0.6 copy.13
Async XLA Ops:
  66.9 1.3 %copy-start = (f32[8,128]{1,0:T(8,128)S(1)}, f32[8,128]{1,0:T(8,128)}, u32[]{:S(2)}) copy-start(f32[8,128]{1,0:T(8,128)} %get-tuple-element.5) | copy-start | bytes 12292

commit v3 on v2

--- a/solution.py
+++ b/solution.py
@@ -154,6 +154,7 @@
         return carry
 
     lax.fori_loop(0, SLOTS, mark, 0)
+    spread(SCALE * start[...], column_spread)
 
     pl.semaphore_wait(barrier, 21)
 
@@ -249,28 +250,39 @@
                         column_major[place] = by_column[columns, rows]
                         row_major[place] = by_row[rows, columns]
 
+    def level(group):
+        for half in (0, 1):
+            tile = 2 * lax.rem(x + (4 - group), 4) + half
+            values = column_tile(tile).astype(jnp.float32)
+            norms = jnp.sum(values * values, axis=1, keepdims=True)
+            column_spread[tile] = column_spread[tile] - SCALE * norms
+
     swap(0)
     ring_turn(2, 0)
     core_copies[0].wait_recv()
     multiply((0, 1, 7), (0,))
-    for turn, x_step in enumerate((1, 3, 2)):
+    level(0)
+    ring_turn(2, 1)
+    ring_turn(2, 2)
+    ring_turn(2, 3)
+    for x_step in (1, 3, 2):
         for step in range(8):
             x_copies[x_step, step].wait_recv()
         swap(x_step)
-        ring_turn(2, turn + 1)
     multiply((2, 6), (0,))
+    ring_turn(3, 0)
     core_copies[1].wait_recv()
     multiply((0, 1, 7), (1,))
-    ring_turn(3, 0)
+    level(1)
+    ring_turn(3, 1)
     core_copies[2].wait_recv()
     multiply((0, 1, 7), (3,))
-    ring_turn(3, 1)
+    level(3)
     core_copies[3].wait_recv()
     multiply((0, 1, 7), (2,))
-    column_norms = tile_norms(column_tile, COLUMN_TILES)
-    spread(SCALE * (start[...] - column_norms), column_spread)
+    level(2)
+    multiply((2, 6), (1, 3, 2))
     ring_turn(3, 2)
-    multiply((2, 6), (1, 2, 3))
     ring_turn(3, 3)
     multiply((3, 5), (0, 1, 2, 3))
     ring_wait(4, 0)
@@ -290,7 +302,7 @@
             )
             return carry
 
-        lax.fori_loop(0, SLOTS, one, 0, unroll=4)
+        lax.fori_loop(0, SLOTS, one, 0, unroll=16)
         slot_peak[...] = slot_peak[...] + jnp.log2(slot_total[...])
 
         shape = bias.shape[1:]
@@ -346,6 +358,8 @@
         copies = exchange(value, x_buf, iteration, corner, corner_peer, x_send, x_recv)
         value = finish(copies, x_buf, iteration)
         copies = exchange(value, z_buf, iteration, z, z_peer, z_send, z_recv)
+        if iteration == 0:
+            column_norms = tile_norms(column_tile, COLUMN_TILES)
         column_level = reference_logs - finish(copies, z_buf, iteration)
         if iteration < ITERS - 1:
             spread(column_level, column_spread)
@@ -356,6 +370,11 @@
         copy.wait_send()
     for copy in [*z_copies.values(), *x_copies.values(), *core_copies]:
         copy.wait_send()
+
+
+def deliver(sample_ref, reference_ref, sample_out, reference_out):
+    sample_out[...] = sample_ref[...]
+    reference_out[...] = reference_ref[...]
 
 
 def body(
@@ -415,6 +434,15 @@
         tile_pairs,
         tile_counts,
     )
+    sample_out, reference_out = pl.pallas_call(
+        deliver,
+        out_shape=(
+            jax.ShapeDtypeStruct((ROW_TILES, TILE), jnp.float32),
+            jax.ShapeDtypeStruct((COLUMN_TILES, TILE), jnp.float32),
+        ),
+        in_specs=[vmem, vmem],
+        out_specs=(vmem, vmem),
+    )(sample_out, reference_out)
     return (sample_out.reshape(-1), reference_out.reshape(-1))
 
 

time: 69 us -> 66.6 us (0.965)
  local copies, waits for them, and re-layouts: 1.89 us -> 0 us
    unnamed x4 -> x0, local copies, waits for them, and re-layouts: 1.89 us -> none
    pallas_call x1, Pallas kernels: 65.6 us -> 63.7 us  [body(): pl.pallas_call(kernel, out_shape=(jax.ShapeDtypeStruct((ROW_TILES, TILE),...]
    pallas_call x0 -> x1, Pallas kernels: none -> 1.3 us  [body(): pl.pallas_call(deliver, out_shape=(jax.ShapeDtypeStruct((ROW_TILES, TILE)...]
where the time goes in v3:
time: 66.6 us; the launch traced here: 66.3 us
  Pallas kernels  65 us (98%)
  between operations  1.29 us (2%)
    pallas_call x1, Pallas kernels, body(): pl.pallas_call(kernel, out_shape=(jax.ShapeDtypeStruct((ROW_TILES, TILE),...  63.7 us

profile of v3, /device:TPU:1, one launch (start us, length us, event | category | flops | bytes accessed | tf_op | source)
XLA Modules:
  0.0 66.3 jit_solution(16162544306247904727)
XLA Ops:
  1.3 63.7 %shard_map.86 = (f32[16,128]{1,0:T(8,128)}, f32[8,128]{1,0:T(8,128)}) custom-call(bf16[256,256]{1,0:T(8,128)(2,1)} %samples.1, bf16[16,256]{1,0:T(8,128)(2,1)} %references.1, f32[16,128]{1,0:T(8,128)} %bitcast.5, f32[8,128]{1,0:T(8,128)} %bitcast.6, f32[8,128]{1,0:T(8,128)} %bitcast.7, s32[1,1,2,48]{3,2,1,0:T(2,128)} %pairs.1, s32[1,1]{1,0:T(1,128)S(6)} %copy.9.counts), custom_call_target="tpu_custom_call" | custom-call | tf_op jit(solution)/shard_map/pallas_call | solution.py:393
  65.0 1.3 %shard_map.87 = (f32[16,128]{1,0:T(8,128)}, f32[8,128]{1,0:T(8,128)}) custom-call(f32[16,128]{1,0:T(8,128)} %get-tuple-element.6.sample_ref, f32[8,128]{1,0:T(8,128)} %get-tuple-element.7.reference_ref), custom_call_target="tpu_custom_call" | custom-call | tf_op jit(solution)/shard_map/pallas_call | solution.py:437

commit v4 on v3

--- a/solution.py
+++ b/solution.py
@@ -290,7 +290,9 @@
     multiply((4,), (0, 1, 2, 3))
 
     def local_pass(products, spread_ref, axis, bias):
-        def one(slot, carry):
+        shape = bias.shape[1:]
+
+        def one(slot, highest):
             row_id = pairs[0, 0, 0, slot]
             column_id = pairs[0, 0, 1, slot]
             place = row_id * COLUMN_TILES + column_id
@@ -300,25 +302,18 @@
             slot_total[pl.ds(slot, 1), :] = jnp.sum(
                 jnp.exp2(scores - peak), axis=0, keepdims=True
             )
-            return carry
-
-        lax.fori_loop(0, SLOTS, one, 0, unroll=16)
-        slot_peak[...] = slot_peak[...] + jnp.log2(slot_total[...])
-
-        shape = bias.shape[1:]
-
-        def highest(slot, peak):
-            return jnp.maximum(peak, slot_peak[pl.ds(slot, 1), :] + bias[slot])
+            return jnp.maximum(highest, peak + bias[slot])
 
         peak = lax.fori_loop(
-            0, SLOTS, highest, jnp.full(shape, LOWEST, jnp.float32), unroll=8
+            0, SLOTS, one, jnp.full(shape, LOWEST, jnp.float32), unroll=48
         )
 
         def collect(slot, total):
-            return total + jnp.exp2(slot_peak[pl.ds(slot, 1), :] + bias[slot] - peak)
+            scale = jnp.exp2(slot_peak[pl.ds(slot, 1), :] + bias[slot] - peak)
+            return total + slot_total[pl.ds(slot, 1), :] * scale
 
         total = lax.fori_loop(
-            0, SLOTS, collect, jnp.zeros(shape, jnp.float32), unroll=8
+            0, SLOTS, collect, jnp.zeros(shape, jnp.float32), unroll=48
         )
         return peak + jnp.log2(total)
 

time: 66.6 us -> 66.2 us (level)
  no operation moved by 1% of the time
where the time goes in v4:
time: 66.2 us; the launch traced here: 66 us
  Pallas kernels  64.7 us (98%)
  between operations  1.29 us (2%)
    pallas_call x1, Pallas kernels, body(): pl.pallas_call(kernel, out_shape=(jax.ShapeDtypeStruct((ROW_TILES, TILE),...  63.4 us

profile of v4, /device:TPU:1, one launch (start us, length us, event | category | flops | bytes accessed | tf_op | source)
XLA Modules:
  0.0 66.0 jit_solution(5878253893419650999)
XLA Ops:
  1.3 63.4 %shard_map.86 = (f32[16,128]{1,0:T(8,128)}, f32[8,128]{1,0:T(8,128)}) custom-call(bf16[256,256]{1,0:T(8,128)(2,1)} %samples.1, bf16[16,256]{1,0:T(8,128)(2,1)} %references.1, f32[16,128]{1,0:T(8,128)} %bitcast.5, f32[8,128]{1,0:T(8,128)} %bitcast.6, f32[8,128]{1,0:T(8,128)} %bitcast.7, s32[1,1,2,48]{3,2,1,0:T(2,128)} %pairs.1, s32[1,1]{1,0:T(1,128)S(6)} %copy.9.counts), custom_call_target="tpu_custom_call" | custom-call | tf_op jit(solution)/shard_map/pallas_call | solution.py:388
  64.7 1.3 %shard_map.87 = (f32[16,128]{1,0:T(8,128)}, f32[8,128]{1,0:T(8,128)}) custom-call(f32[16,128]{1,0:T(8,128)} %get-tuple-element.6.sample_ref, f32[8,128]{1,0:T(8,128)} %get-tuple-element.7.reference_ref), custom_call_target="tpu_custom_call" | custom-call | tf_op jit(solution)/shard_map/pallas_call | solution.py:432

commit v5 on v4

--- a/solution.py
+++ b/solution.py
@@ -143,19 +143,6 @@
     for copy in own_copies:
         copy.start()
 
-    in_use = counts[0, 0]
-    row_place = lax.broadcasted_iota(jnp.int32, (ROW_TILES, TILE), 0)
-    column_place = lax.broadcasted_iota(jnp.int32, (COLUMN_TILES, TILE), 0)
-
-    def mark(slot, carry):
-        spare = jnp.where(slot < in_use, 0.0, LOWEST).astype(jnp.float32)
-        row_bias[slot] = jnp.where(row_place == pairs[0, 0, 0, slot], spare, LOWEST)
-        column_bias[slot] = jnp.where(column_place == pairs[0, 0, 1, slot], spare, LOWEST)
-        return carry
-
-    lax.fori_loop(0, SLOTS, mark, 0)
-    spread(SCALE * start[...], column_spread)
-
     pl.semaphore_wait(barrier, 21)
 
     def gather(source, target, index, device):
@@ -211,6 +198,19 @@
     for turn in range(PIECES):
         ring_start(1, turn)
     forward(0)
+
+    in_use = counts[0, 0]
+    row_place = lax.broadcasted_iota(jnp.int32, (ROW_TILES, TILE), 0)
+    column_place = lax.broadcasted_iota(jnp.int32, (COLUMN_TILES, TILE), 0)
+
+    def mark(slot, carry):
+        spare = jnp.where(slot < in_use, 0.0, LOWEST).astype(jnp.float32)
+        row_bias[slot] = jnp.where(row_place == pairs[0, 0, 0, slot], spare, LOWEST)
+        column_bias[slot] = jnp.where(column_place == pairs[0, 0, 1, slot], spare, LOWEST)
+        return carry
+
+    lax.fori_loop(0, SLOTS, mark, 0)
+    spread(SCALE * start[...], column_spread)
 
     for turn, steps in enumerate(((1, 7), (2, 6), (3, 5), (4,))):
         for step in steps:

time: 66.2 us -> 66.3 us (level)
  no operation moved by 1% of the time
where the time goes in v5:
time: 66.3 us; the launch traced here: 66 us
  Pallas kernels  64.7 us (98%)
  between operations  1.29 us (2%)
    pallas_call x1, Pallas kernels, body(): pl.pallas_call(kernel, out_shape=(jax.ShapeDtypeStruct((ROW_TILES, TILE),...  63.4 us

profile of v5, /device:TPU:1, one launch (start us, length us, event | category | flops | bytes accessed | tf_op | source)
XLA Modules:
  0.0 66.0 jit_solution(8672581246005379197)
XLA Ops:
  1.3 63.4 %shard_map.86 = (f32[16,128]{1,0:T(8,128)}, f32[8,128]{1,0:T(8,128)}) custom-call(bf16[256,256]{1,0:T(8,128)(2,1)} %samples.1, bf16[16,256]{1,0:T(8,128)(2,1)} %references.1, f32[16,128]{1,0:T(8,128)} %bitcast.5, f32[8,128]{1,0:T(8,128)} %bitcast.6, f32[8,128]{1,0:T(8,128)} %bitcast.7, s32[1,1,2,48]{3,2,1,0:T(2,128)} %pairs.1, s32[1,1]{1,0:T(1,128)S(6)} %copy.9.counts), custom_call_target="tpu_custom_call" | custom-call | tf_op jit(solution)/shard_map/pallas_call | solution.py:388
  64.7 1.3 %shard_map.87 = (f32[16,128]{1,0:T(8,128)}, f32[8,128]{1,0:T(8,128)}) custom-call(f32[16,128]{1,0:T(8,128)} %get-tuple-element.6.sample_ref, f32[8,128]{1,0:T(8,128)} %get-tuple-element.7.reference_ref), custom_call_target="tpu_custom_call" | custom-call | tf_op jit(solution)/shard_map/pallas_call | solution.py:432
